TPU v7x, 32 devices: a whole 2x2x4 slice. The times are simulated.
32 devices in a mesh: groups: 2 (over x), seq: 16 (over z, y, core).
Axes of the slice: x: 2, y: 2, z: 4, core: 2. Of those that a mesh axis runs over, the one named last changes fastest.
Arguments:
- layer_in: bfloat16 [8192, 2560], P(('groups', 'seq')), parts along dimension 0, may hold values from -6 to 6
- ssm_in: bfloat16 [8192, 2560], P(('groups', 'seq')), parts along dimension 0, may hold values from -6 to 6
- weight_bc: bfloat16 [2560, 256], replicated, may hold values from -0.015625 to 0.015625
- weight_dt: bfloat16 [2560, 40], replicated, may hold values from -0.125 to 0.125
- bias_dt: float32 [40], replicated, may hold values from -3 to 0.5
- log_rate: float32 [40], replicated, may hold values from -13.2 to -2.9
- skip_gain: float32 [40], replicated, may hold values from 0.5 to 1.5
- grad_out: bfloat16 [8192, 2560], P(('groups', 'seq')), parts along dimension 0, may hold values from -8 to 8
Outputs:
- grad_ssm_in: bfloat16 [8192, 2560], P(('groups', 'seq')), parts along dimension 0
- grad_layer_in: bfloat16 [8192, 2560], P(('groups', 'seq')), parts along dimension 0
- grad_weight_bc: float32 [5120, 256], P(('groups', 'seq')), parts along dimension 0
- grad_weight_dt: float32 [5120, 40], P(('groups', 'seq')), parts along dimension 0
- grad_bias_dt: float32 [80], P('groups'), parts along dimension 0
- grad_log_rate: float32 [80], P('groups'), parts along dimension 0
- grad_skip_gain: float32 [80], P('groups'), parts along dimension 0
There are 2 independent parts, one for each index of `groups`. A program takes and returns all parts, laid end to end along the dimension named above; an argument that names none is the same for every part. Nothing has to cross between parts.
All inputs are finite; a program needn't handle non-finite values.
Results may differ from a plain program's by a relative error of at most 0.0059.
Values sent between devices are 32-bit elements; how exact they have to be, the bound alone decides.
A program may use at most 128 MiB of HBM per device.

v0:
```python
import jax
import jax.numpy as jnp
from jax import lax
from jax.sharding import PartitionSpec as P

BLOCK = 256


HIGHEST = lax.Precision.HIGHEST


def block_pass(carry, pieces):
    state, offset = carry
    values, b_rows, c_rows, scores, step_size, log_decay = pieces
    running = jnp.cumsum(log_decay, axis=0)
    count = values.shape[0]
    indices = jnp.arange(count)
    lower_mask = indices[:, None] >= indices[None, :]
    run_heads = running.T
    spread = jnp.where(
        lower_mask[None, :, :], run_heads[:, :, None] - run_heads[:, None, :], -jnp.inf
    )
    mixing = jnp.exp(spread) * scores[None, :, :] * step_size.T[:, None, :]
    inner = jnp.einsum("hts,shp->thp", mixing, values, precision=HIGHEST)
    carried = jnp.exp(running)[:, :, None] * jnp.einsum(
        "tn,hpn->thp", c_rows, state, precision=HIGHEST
    )
    tail_weight = jnp.exp(running[-1][None, :] - running) * step_size
    fresh = jnp.einsum("shp,sn->hpn", tail_weight[:, :, None] * values, b_rows, precision=HIGHEST)
    new_state = jnp.exp(running[-1])[:, None, None] * state + fresh
    leading = jnp.exp(running + offset[None, :])
    return ((new_state, offset + running[-1]), (inner + carried, leading))


def local_part(values, b_rows, c_rows, scores, step_raw, log_rate):
    step_size = jax.nn.softplus(step_raw)
    log_decay = -jnp.exp(log_rate)[None, :] * step_size
    blocks = values.shape[0] // BLOCK

    def split(array):
        return array.reshape((blocks, BLOCK) + array.shape[1:])

    start = (
        jnp.zeros((values.shape[1], values.shape[2], b_rows.shape[1]), jnp.float32),
        jnp.zeros((values.shape[1],), jnp.float32),
    )
    finals, outputs = lax.scan(
        jax.checkpoint(block_pass),
        start,
        (split(values), split(b_rows), split(c_rows), scores, split(step_size), split(log_decay)),
    )
    local_state, log_total = finals
    mixed_part, leading = outputs
    return (
        mixed_part.reshape(values.shape),
        local_state,
        log_total,
        leading.reshape(step_size.shape),
    )


def across_devices(log_pieces, state_pieces, flip):
    logs = log_pieces[:, :, 0]
    through = jnp.cumsum(logs, axis=1)
    before = through - logs
    count = logs.shape[1]
    indices = jnp.arange(count)
    if flip:
        spread = before[:, None, :] - through[:, :, None]
        valid = indices[None, :] > indices[:, None]
    else:
        spread = before[:, :, None] - through[:, None, :]
        valid = indices[None, :] < indices[:, None]
    weights = jnp.exp(jnp.where(valid[None, :, :], spread, -jnp.inf))
    return jnp.einsum("hij,hjm->him", weights, state_pieces, precision=HIGHEST)


def contract_rows(left, right):
    return lax.dot_general(
        left, right, (((1,), (1,)), ((), ())), preferred_element_type=jnp.float32
    )


def local(layer_in, ssm_in, weight_bc, weight_dt, bias_dt, log_rate, skip_gain, grad_out):
    tokens = layer_in.shape[0]
    heads = log_rate.shape[0]
    state_dim = weight_bc.shape[1] // 2
    head_size = ssm_in.shape[1] // heads
    devices = lax.axis_size("seq")
    blocks = tokens // BLOCK
    proj_bc = jnp.dot(layer_in, weight_bc, preferred_element_type=jnp.float32).astype(jnp.bfloat16)
    proj_kept = lax.optimization_barrier(proj_bc)
    proj_wide = proj_kept.astype(jnp.float32)
    b_rows = proj_wide[:, :state_dim]
    c_rows = proj_wide[:, state_dim:]
    b_narrow = proj_kept[:, :state_dim].reshape(blocks, BLOCK, state_dim)
    c_narrow = proj_kept[:, state_dim:].reshape(blocks, BLOCK, state_dim)
    scores = jnp.einsum("ktn,ksn->kts", c_narrow, b_narrow, preferred_element_type=jnp.float32)
    step_raw = jnp.dot(layer_in, weight_dt, preferred_element_type=jnp.float32) + bias_dt[None, :]
    values = ssm_in.astype(jnp.float32).reshape(tokens, heads, head_size)
    cotangent = grad_out.astype(jnp.float32).reshape(tokens, heads, head_size)
    primal, pull = jax.vjp(local_part, values, b_rows, c_rows, scores, step_raw, log_rate)
    mixed_part, local_state, log_total, leading = primal
    scaled_grad = leading[:, :, None] * cotangent
    state_grad = jnp.einsum("thp,tn->hpn", scaled_grad, c_rows, precision=HIGHEST)
    share = head_size * state_dim // devices
    log_copies = jnp.broadcast_to(log_total[:, None, None], (heads, devices, 1))
    packed = jnp.concatenate(
        [local_state.reshape(heads, devices, share), state_grad.reshape(heads, devices, share)],
        axis=2,
    )
    pieces = (
        lax.all_to_all(log_copies, "seq", split_axis=1, concat_axis=1, tiled=True),
        lax.all_to_all(packed, "seq", split_axis=1, concat_axis=1, tiled=True),
    )
    half = pieces[1].shape[2] // 2
    prefix = across_devices(pieces[0], pieces[1][:, :, :half], False)
    suffix = across_devices(pieces[0], pieces[1][:, :, half:], True)
    joined = jnp.concatenate([prefix, suffix], axis=2)
    returned = lax.all_to_all(joined, "seq", split_axis=1, concat_axis=1, tiled=True)
    incoming = returned[:, :, :share].reshape(heads, head_size, state_dim)
    outgoing = returned[:, :, share:].reshape(heads, head_size, state_dim)
    read_out = jnp.einsum("tn,hpn->thp", c_rows, incoming, precision=HIGHEST)
    grad_leading = jnp.sum(cotangent * read_out, axis=2)
    grad_c_extra = jnp.einsum("thp,hpn->tn", scaled_grad, incoming, precision=HIGHEST)
    grad_log_total = jnp.exp(log_total) * jnp.sum(outgoing * incoming, axis=(1, 2))
    grad_values, grad_b, grad_c, grad_scores, grad_step, grad_log_rate = pull(
        (cotangent, outgoing, grad_log_total, grad_leading)
    )
    b_blocks = b_rows.reshape(blocks, BLOCK, state_dim)
    c_blocks = c_rows.reshape(blocks, BLOCK, state_dim)
    grad_b = grad_b + jnp.einsum("kts,ktn->ksn", grad_scores, c_blocks, precision=HIGHEST).reshape(
        tokens, state_dim
    )
    grad_c = (
        grad_c
        + grad_c_extra
        + jnp.einsum("kts,ksn->ktn", grad_scores, b_blocks, precision=HIGHEST).reshape(
            tokens, state_dim
        )
    )
    grad_values = grad_values + skip_gain[None, :, None] * cotangent
    grad_skip_local = jnp.sum(values * cotangent, axis=(0, 2))
    grad_bias_dt, grad_log_rate, grad_skip_gain = lax.psum(
        (jnp.sum(grad_step, axis=0), grad_log_rate, grad_skip_local), "seq"
    )
    grad_proj = jnp.concatenate([grad_b, grad_c, grad_step], axis=1).astype(jnp.bfloat16)
    grad_layer_in = (
        contract_rows(grad_proj[:, : 2 * state_dim], weight_bc)
        + contract_rows(grad_proj[:, 2 * state_dim :], weight_dt)
    ).astype(jnp.bfloat16)
    weight_rows = lax.psum_scatter(
        lax.dot_general(
            layer_in, grad_proj, (((0,), (0,)), ((), ())), preferred_element_type=jnp.float32
        ),
        "seq",
        scatter_dimension=0,
        tiled=True,
    )
    grad_weight_bc = weight_rows[:, : 2 * state_dim]
    grad_weight_dt = weight_rows[:, 2 * state_dim :]
    grad_ssm_in = grad_values.reshape(tokens, heads * head_size).astype(jnp.bfloat16)
    return (
        grad_ssm_in,
        grad_layer_in,
        grad_weight_bc,
        grad_weight_dt,
        grad_bias_dt,
        grad_log_rate,
        grad_skip_gain,
    )


def solution(mesh):
    in_specs = (
        P(("groups", "seq"), None),
        P(("groups", "seq"), None),
        P(),
        P(),
        P(),
        P(),
        P(),
        P(("groups", "seq"), None),
    )
    out_specs = (
        P(("groups", "seq"), None),
        P(("groups", "seq"), None),
        P(("groups", "seq"), None),
        P(("groups", "seq"), None),
        P("groups"),
        P("groups"),
        P("groups"),
    )
    return jax.shard_map(local, mesh=mesh, in_specs=in_specs, out_specs=out_specs, check_vma=False)
```

profile of v0, /device:TPU:0, one launch (start us, length us, event | category | flops | bytes accessed | tf_op | source)
XLA Modules:
  0.0 352.9 jit_solution(839638582217675029)
XLA Ops:
  11.6 7.4 %all-to-all-start = ((f32[40,16,1]{0,2,1:T(1,128)}), f32[40,16,1]{0,2,1:T(1,128)S(1)}, u32[]{:S(2)}, u32[]{:S(2)}) async-start(f32[40,16,1]{0,2,1:T(1,128)} %broadcast_in_dim.129), calls=%async_computation | async-start | bytes 16384 | tf_op jit(solution)/shard_map/all_to_all | solution.py:113
  19.1 1.8 convolution_convert_fusion
  21.2 1.6 copy.146
  22.8 2.4 copy.138
  25.2 2.5 fusion.21
  27.7 2.5 reshape.265
  30.2 3.2 copy.148
  33.4 2.0 multiply_reduce_fusion.2
  35.5 2.4 convolution_add_fusion.1
  37.8 2.5 reshape.263
  40.3 2.2 copy.147
  42.5 1.7 pad_maximum_fusion
  44.3 6.5 %all-to-all-start.1 = ((f32[40,16,1024]{2,0,1:T(8,128)}), f32[40,16,1024]{2,0,1:T(8,128)}, u32[]{:S(2)}, u32[]{:S(2)}) async-start(f32[40,16,1024]{2,0,1:T(8,128)} %pad_maximum_fusion), calls=%async_computation.1 | async-start | bytes 5242880 | tf_op jit(solution)/shard_map/all_to_all | solution.py:114
  51.1 49.8 %all-to-all-done.1 = f32[40,16,1024]{2,0,1:T(8,128)} async-done(((f32[40,16,1024]{2,0,1:T(8,128)}), f32[40,16,1024]{2,0,1:T(8,128)}, u32[]{:S(2)}, u32[]{:S(2)}) %all-to-all-start.1) | async-done | bytes 2621472 | tf_op jit(solution)/shard_map/all_to_all | solution.py:114
  101.0 1.9 fusion.103
  102.9 1.9 fusion.29
  104.8 1.9 fusion.27
  107.0 3.0 copy.151
  110.0 13.4 %all-to-all-start.2 = ((f32[40,16,1024]{2,0,1:T(8,128)}), f32[40,16,1024]{2,0,1:T(8,128)}, u32[]{:S(2)}, u32[]{:S(2)}) async-start(f32[40,16,1024]{2,0,1:T(8,128)} %copy.151), calls=%async_computation.2 | async-start | bytes 5242880 | tf_op jit(solution)/shard_map/all_to_all | solution.py:120
  123.6 1.9 convert.12
  125.5 1.8 convert.11
  128.9 44.6 %all-to-all-done.2 = f32[40,16,1024]{2,0,1:T(8,128)} async-done(((f32[40,16,1024]{2,0,1:T(8,128)}), f32[40,16,1024]{2,0,1:T(8,128)}, u32[]{:S(2)}, u32[]{:S(2)}) %all-to-all-start.2) | async-done | bytes 2621472 | tf_op jit(solution)/shard_map/all_to_all | solution.py:120
  173.6 3.2 fusion.102
  177.3 1.8 copy.153
  179.1 2.4 reshape.267
  181.5 2.6 multiply_reduce_fusion.5
  184.1 4.4 %convolution_bitcast_fusion.1 = f32[256,128]{0,1:T(8,128)S(1)} fusion(f32[256,40,64]{0,2,1:T(8,128)} %bitcast.154, f32[40,64,128]{2,1,0:T(8,128)S(1)} %copy-done.5), kind=kOutput, calls=%fused_computation.52 | convolution fusion | flops 1006632960 | bytes 4063232 | tf_op jit(solution)/shard_map/thp,hpn->tn/dot_general | solution.py:125
  188.5 1.8 copy.152
  190.4 2.3 reshape.266
  195.3 2.8 multiply_reduce_fusion.6
  198.1 2.3 multiply_reduce_fusion.3
  201.9 18.8 %fusion.5 = (f32[40,256]{1,0:T(8,128)}, f32[40,256]{1,0:T(8,128)}, f32[40,256]{1,0:T(8,128)}, f32[256,256]{1,0:T(8,128)S(1)}) fusion(f32[40,256]{1,0:T(8,128)} %copy.159, f32[256,256]{1,0:T(8,128)} %fusion.87, f32[40,256]{1,0:T(8,128)} %copy.157, pred[256,256]{1,0:T(8,128)(4,1)} %iota_compare_fusion, f32[256,40,64]{0,2,1:T(8,128)} %convert.11, ...), kind=kOutput, calls=%fused_computation.8 | convolution fusion | flops 2047248384 | bytes 6037504 | tf_op jit(solution)/shard_map/transpose(jvp())/while/body/eval_jaxpr/checkpoint/hts,shp->thp/dot_general | solution.py:24
  220.7 1.5 copy.166
  223.8 1.5 copy.162
  225.3 6.4 %multiply_reduce_fusion.4 = (f32[256,40]{0,1:T(8,128)}, f32[256,40,64]{0,2,1:T(8,128)}) fusion(f32[256,40,64]{0,2,1:T(8,128)} %convert.11, f32[40,64,128]{2,1,0:T(8,128)} %reshape.266, f32[256,128]{1,0:T(8,128)S(1)} %get-tuple-element.89), kind=kOutput, calls=%fused_computation.30 | convolution fusion | flops 1007933440 | bytes 6725632 | tf_op jit(solution)/shard_map/transpose(jvp())/while/body/eval_jaxpr/checkpoint/shp,sn->hpn/dot_general | solution.py:29
  233.4 1.9 bitcast_add_fusion.2
  236.3 2.8 reduce-window.26
  240.2 5.2 %fusion.34 = f32[256,128]{0,1:T(8,128)} fusion(f32[40,64,128]{2,1,0:T(8,128)} %reshape.266, f32[256,40,64]{0,2,1:T(8,128)} %convert.11, f32[256,40]{0,1:T(8,128)S(1)} %copy.156), kind=kOutput, calls=%fused_computation.49 | convolution fusion | flops 1007288320 | bytes 4104192 | tf_op jit(solution)/shard_map/transpose(jvp())/while/body/eval_jaxpr/checkpoint/shp,sn->hpn/dot_general | solution.py:29
  246.2 2.4 fusion.100
  250.8 4.5 %fusion.40 = f32[256,128]{0,1:T(8,128)S(1)} fusion(f32[256,128]{0,1:T(8,128)S(1)} %convolution_bitcast_fusion.1, f32[40,64,128]{2,1,0:T(8,128)} %copy-done.2, f32[256,40,64]{0,2,1:T(8,128)} %convert.12, f32[256,40]{0,1:T(8,128)S(1)} %copy.160), kind=kOutput, calls=%fused_computation.55 | convolution fusion | flops 1007321088 | bytes 4235264 | tf_op jit(solution)/shard_map/transpose(jvp())/while/body/eval_jaxpr/checkpoint/tn,hpn->thp/dot_general | solution.py:25
  255.6 2.2 convolution_bitcast_fusion
  257.8 5.0 %copy.174 = f32[2560,296]{1,0:T(8,128)} copy(f32[2560,296]{0,1:T(8,128)} %convolution_bitcast_fusion) | data formatting | bytes 6062080
  263.9 10.8 %bitcast_add_fusion.1 = f32[256,40,64]{0,2,1:T(8,128)S(1)} fusion(f32[256,40,64]{0,2,1:T(8,128)} %get-tuple-element.199, f32[40,256]{1,0:T(8,128)S(1)} %copy-done.15, f32[256,256]{1,0:T(8,128)S(1)} %copy-done.10, f32[40,256]{1,0:T(8,128)S(1)} %copy-done.16, pred[256,256]{1,0:T(8,128)(4,1)S(1)} %copy-done.14, f32[256,40,64]{0,2,1:T(8,128)} %convert.12, ...), kind=kOutput, calls=%fused_computation.23 | convolution fusion | flops 2025062400 | bytes 8314880 | tf_op jit(solution)/shard_map/transpose(jvp())/while/body/eval_jaxpr/checkpoint/hts,shp->thp/dot_general | solution.py:24
  276.1 2.6 copy.171
  278.8 42.5 %all-reduce.3 = (f32[40]{0:T(128)}, f32[40]{0:T(128)}, f32[40]{0:T(128)}) all-reduce(f32[40]{0:T(128)S(1)} %copy-done.20, f32[40]{0:T(128)S(1)} %negate_multiply_fusion, f32[40]{0:T(128)S(1)} %reduce_sum.203), channel_id=1, replica_groups=mesh['groups'=2,'seq'=16] {'seq'}, use_global_device_ids=true, to_apply=%region_19.20 | all-reduce | flops 120 | bytes 960 | tf_op jit(solution)/shard_map/psum | solution.py:144
  321.8 1.5 fusion.12
  323.4 19.1 %reduce-scatter.4.cloned.1.call-done = f32[160,296]{1,0:T(8,128)} async-done(((f32[2560,296]{1,0:T(8,128)}), f32[160,296]{1,0:T(8,128)}) %reduce-scatter.4.cloned.1.call-update) | async-done | bytes 189456
  344.1 1.6 slice.96
  (112 shorter events, 24.9 us)
Async XLA Ops:
  7.2 1.3 copy-start
  8.5 12.4 %copy-start.17 = (f32[40]{0:T(128)}, f32[40]{0:T(128)S(1)}, u32[]{:S(2)}) copy-start(f32[40]{0:T(128)S(1)} %exponential_negate_fusion) | copy-start | bytes 484
  10.0 11.2 %copy-start.9 = (f32[256,40]{1,0:T(8,128)}, f32[256,40]{1,0:T(8,128)S(1)}, u32[]{:S(2)}) copy-start(f32[256,40]{1,0:T(8,128)S(1)} %get-tuple-element.197) | copy-start | bytes 122884
  11.6 32.6 %all-to-all-start = ((f32[40,16,1]{0,2,1:T(1,128)}), f32[40,16,1]{0,2,1:T(1,128)S(1)}, u32[]{:S(2)}, u32[]{:S(2)}) async-start(f32[40,16,1]{0,2,1:T(1,128)} %broadcast_in_dim.129), calls=%async_computation | async-start | bytes 16384 | tf_op jit(solution)/shard_map/all_to_all | solution.py:113
  30.2 3.2 copy-start.3
  40.3 2.2 copy-start.6
  44.3 56.7 %all-to-all-start.1 = ((f32[40,16,1024]{2,0,1:T(8,128)}), f32[40,16,1024]{2,0,1:T(8,128)}, u32[]{:S(2)}, u32[]{:S(2)}) async-start(f32[40,16,1024]{2,0,1:T(8,128)} %pad_maximum_fusion), calls=%async_computation.1 | async-start | bytes 5242880 | tf_op jit(solution)/shard_map/all_to_all | solution.py:114
  110.0 63.5 %all-to-all-start.2 = ((f32[40,16,1024]{2,0,1:T(8,128)}), f32[40,16,1024]{2,0,1:T(8,128)}, u32[]{:S(2)}, u32[]{:S(2)}) async-start(f32[40,16,1024]{2,0,1:T(8,128)} %copy.151), calls=%async_computation.2 | async-start | bytes 5242880 | tf_op jit(solution)/shard_map/all_to_all | solution.py:120
  123.4 219.1 %reduce-scatter.4.cloned.1.call-start = ((), (), s32[]{:S(2)}) async-start(), calls=%async_computation.4 | async-start | bytes 4177920
  123.6 1.9 copy-start.4
  181.5 2.7 copy-start.5
  184.1 4.4 %copy-start.7 = (f32[40,16,512]{2,0,1:T(8,128)S(1)}, f32[40,16,512]{2,0,1:T(8,128)}, u32[]{:S(2)}) copy-start(f32[40,16,512]{2,0,1:T(8,128)} %get-tuple-element.178) | copy-start | bytes 3932164
  195.1 3.0 copy-start.1
  195.3 2.8 copy-start.2
  235.3 10.9 %copy-start.18 = (f32[40]{0:T(128)S(1)}, f32[40]{0:T(128)}, u32[]{:S(2)}) copy-start(f32[40]{0:T(128)} %copy-done.17) | copy-start | bytes 484
  240.2 5.2 %copy-start.12 = (f32[256,40]{0,1:T(8,128)}, f32[256,40]{0,1:T(8,128)S(1)}, u32[]{:S(2)}) copy-start(f32[256,40]{0,1:T(8,128)S(1)} %copy.156) | copy-start | bytes 122884
  262.8 0.7 copy-start.19
  262.8 1.0 copy-start.10
  262.8 1.0 copy-start.13
  262.8 1.0 copy-start.14
  262.8 1.0 copy-start.15
  262.8 1.0 copy-start.16
  276.1 2.7 copy-start.21
  276.1 2.7 copy-start.22
  276.1 2.7 copy-start.20
  276.1 45.2 %copy-start.8 = (bf16[2560,256]{1,0:T(8,128)(2,1)S(1)}, bf16[2560,256]{1,0:T(8,128)(2,1)}, u32[]{:S(2)}) copy-start(bf16[2560,256]{1,0:T(8,128)(2,1)} %param.10) | copy-start | bytes 3932164
  278.7 43.1 %copy-start.11 = (bf16[2560,40]{0,1:T(8,128)(2,1)S(1)}, bf16[2560,40]{0,1:T(8,128)(2,1)}, u32[]{:S(2)}) copy-start(bf16[2560,40]{0,1:T(8,128)(2,1)} %param.11) | copy-start | bytes 614404
Sparse Core Ops, SparseCore 0:
  263.0 79.4 reduce-scatter.3
where the time goes:
time: 360 us; the launch traced here: 353 us
  waiting for transfers between devices  114 us (32%)
  matrix products  73.7 us (20%)
  local copies, waits for them, and re-layouts  54 us (15%)
  blocking collectives  42.5 us (12%)
  starting transfers between devices  27.5 us (8%)
  other arithmetic  26.8 us (7%)
  between operations  14.9 us (4%)
    all_to_all x1, waiting for transfers between devices, local(): lax.all_to_all(packed, 'seq', split_axis=1, concat_axis=1, tiled=True)  49.8 us
    all_to_all x1, waiting for transfers between devices, local(): lax.all_to_all(joined, 'seq', split_axis=1, concat_axis=1, tiled=True)  44.6 us
    psum x1, blocking collectives, local(): lax.psum((jnp.sum(grad_step, axis=0), grad_log_rate, grad_skip_local), 's...  42.5 us
    dot_general x2, matrix products, block_pass(): inner = jnp.einsum('hts,shp->thp', mixing, values, precision=HIGHEST)  29.6 us
    unnamed x2, waiting for transfers between devices  19.1 us
    dot_general x3, matrix products, block_pass(): jnp.einsum('shp,sn->hpn', tail_weight[:, :, None] * values, b_rows, preci...  14 us
    unnamed x51, local copies, waits for them, and re-layouts  13.6 us
    all_to_all x1, starting transfers between devices, local(): lax.all_to_all(joined, 'seq', split_axis=1, concat_axis=1, tiled=True)  13.4 us
  transfers between devices with their start and end apart: 4, of which 3 were waited for; matrix products, arithmetic and copies ran while one was open for 14% of the time, Pallas kernels for 0%

commit v1 on v0

v1 whole, which is shorter than its diff:
```python
import functools
import jax
import jax.numpy as jnp
from jax import lax
from jax.experimental import pallas as pl
from jax.experimental.pallas import tpu as pltpu
from jax.sharding import PartitionSpec as P

F32 = jnp.float32
BF16 = jnp.bfloat16
TILE = 128
CHUNKS = 4
VMEM_LIMIT = 60 * 1024 * 1024
VMEM = pl.BlockSpec(memory_space=pltpu.VMEM)


def mm(left, right):
    return lax.dot_general(left, right, (((1,), (0,)), ((), ())), preferred_element_type=F32)


def mm_nt(left, right):
    return lax.dot_general(left, right, (((1,), (1,)), ((), ())), preferred_element_type=F32)


def mm_tn(left, right):
    return lax.dot_general(left, right, (((0,), (0,)), ((), ())), preferred_element_type=F32)


def three_way(x):
    high = x.astype(BF16)
    rest = x - high.astype(F32)
    middle = rest.astype(BF16)
    return high, middle, (rest - middle.astype(F32)).astype(BF16)


def one_hot(heads, width, columns, first=0):
    row = lax.broadcasted_iota(jnp.int32, (heads, columns), 0)
    col = lax.broadcasted_iota(jnp.int32, (heads, columns), 1) + first
    inside = (col >= row * width) & (col < (row + 1) * width)
    return jnp.where(inside, 1.0, 0.0).astype(BF16)


def spread_heads(x, hot):
    parts = three_way(x)
    return mm(parts[0], hot) + mm(parts[1], hot) + mm(parts[2], hot)


def head_sum(x, hot):
    high = x.astype(BF16)
    low = (x - high.astype(F32)).astype(BF16)
    return mm_nt(high, hot) + mm_nt(low, hot)


def exact_mm(mask, x):
    parts = three_way(x)
    return mm(mask, parts[0]) + mm(mask, parts[1]) + mm(mask, parts[2])


def triangle(size, compare):
    row = lax.broadcasted_iota(jnp.int32, (size, size), 0)
    col = lax.broadcasted_iota(jnp.int32, (size, size), 1)
    return jnp.where(compare(row, col), 1.0, 0.0).astype(BF16)


def before_kernel(
    layer_ref, values_ref, wbc_ref, wdt_ref, bias_ref, rate_ref, grad_ref,
    proj_ref, raw_ref, run_ref, run_rows_ref, states_ref, total_ref, scores_ref, skip_ref,
    u_ref, runx_ref,
):
    tokens = layer_ref.shape[0]
    heads = bias_ref.shape[1]
    width = values_ref.shape[1]
    head_size = width // heads
    state_dim = wbc_ref.shape[1] // 2
    layer = layer_ref[...]
    proj = mm(layer, wbc_ref[...]).astype(BF16)
    proj_ref[...] = proj
    b_rows = proj[:, :state_dim]
    c_rows = proj[:, state_dim:]
    scores_ref[...] = mm_nt(b_rows, c_rows)
    raw = mm(layer, wdt_ref[...]) + bias_ref[...]
    raw_ref[...] = raw
    step = jnp.maximum(raw, 0.0) + jnp.log1p(jnp.exp(-jnp.abs(raw)))
    decay = -jnp.exp(rate_ref[...]) * step
    run = exact_mm(triangle(tokens, lambda r, c: r >= c), decay)
    run_ref[...] = run
    run_rows = run.T
    for head in range(heads):
        run_rows_ref[head] = run_rows[head : head + 1]
    total = run[tokens - 1 :, :]
    total_ref[...] = jnp.zeros_like(total_ref)
    total_ref[:, :heads] = jnp.broadcast_to(total, (total_ref.shape[0], heads))
    hot = one_hot(heads, head_size, width)
    values = values_ref[...].astype(F32)
    grad = grad_ref[...].astype(F32)
    u_ref[...] = (spread_heads(step, hot) * values).astype(BF16)
    tail = spread_heads(jnp.exp(total - run) * step, hot)
    states_ref[0] = mm_tn(b_rows, (tail * values).astype(BF16))
    lead = spread_heads(jnp.exp(run), hot)
    states_ref[1] = mm_tn(c_rows, (lead * grad).astype(BF16))
    products = jnp.sum(values * grad, axis=0, keepdims=True)
    skip_ref[...] = head_sum(jnp.broadcast_to(products, (8, width)), hot)
    wide = one_hot(heads, TILE, heads * TILE)
    runx_ref[...] = spread_heads(run, wide)


def inner_pair(pair, values_ref, u_ref, grad_ref, scores_ref, runx_ref, run_rows_ref,
               gu_ref, rows_ref, gscores_ref, head_size):
    tokens = u_ref.shape[0]
    blocks = tokens // TILE
    per = TILE // head_size
    cols = pl.ds(pl.multiple_of(pair * TILE, TILE), TILE)
    lane = lax.broadcasted_iota(jnp.int32, (TILE, TILE), 1)
    causal = lax.broadcasted_iota(jnp.int32, (TILE, TILE), 0) <= lane
    grads = [grad_ref[t * TILE : (t + 1) * TILE, cols] for t in range(blocks)]
    gus = [jnp.zeros((TILE, TILE), F32) for _ in range(blocks)]
    for sub in range(per):
        head = pair * per + sub
        keep = (lane >= sub * head_size) & (lane < (sub + 1) * head_size)
        hcols = pl.ds(pl.multiple_of(head * TILE, TILE), TILE)
        rows = [jnp.zeros((1, TILE), F32) for _ in range(blocks)]
        for s in range(blocks):
            srange = slice(s * TILE, (s + 1) * TILE)
            run_col = runx_ref[srange, hcols]
            u_head = jnp.where(keep, u_ref[srange, cols], jnp.zeros((), BF16))
            gu = jnp.zeros((TILE, TILE), F32)
            for t in range(s, blocks):
                trange = slice(t * TILE, (t + 1) * TILE)
                gap = run_rows_ref[head, :, trange] - run_col
                if s == t:
                    gap = jnp.where(causal, gap, -jnp.inf)
                factor = jnp.exp(gap)
                mixing = (factor * scores_ref[srange, trange]).astype(BF16)
                weight = mm_nt(u_head, grads[t])
                gscores_ref[srange, trange] += factor * weight
                rows[t] += jnp.sum(mixing.astype(F32) * weight, axis=0, keepdims=True)
                gu += mm(mixing, grads[t])
            gus[s] = jnp.where(keep, gu, gus[s])
        for t in range(blocks):
            rows_ref[head, :, t * TILE : (t + 1) * TILE] = rows[t]
    for s in range(blocks):
        gu_ref[s * TILE : (s + 1) * TILE, cols] = gus[s]


def inner_kernel(head_size, u_ref, grad_ref, scores_ref, runx_ref, run_rows_ref,
                 gu_ref, rows_ref, gscores_ref):
    gscores_ref[...] = jnp.zeros_like(gscores_ref)

    def body(pair, _):
        inner_pair(pair, None, u_ref, grad_ref, scores_ref, runx_ref, run_rows_ref,
                   gu_ref, rows_ref, gscores_ref, head_size)
        return 0

    lax.fori_loop(0, u_ref.shape[1] // TILE, body, 0)


def scan_plan(devices, rows):
    levels = devices.bit_length() - 1
    sizes, halved = [rows], []
    for level in range(levels - 1):
        cut = sizes[-1] >= 16
        halved.append(cut)
        sizes.append(sizes[-1] // 2 if cut else sizes[-1])
    return levels, sizes, halved


def scan_kernel(devices, heads, states_ref, total_ref, out_ref, *refs):
    rows, width = states_ref.shape[1], states_ref.shape[2]
    head_size = width // heads
    levels, sizes, halved = scan_plan(devices, rows)
    top = levels - 1
    refs = list(refs)
    aggs = [states_ref] + [refs.pop(0) for _ in range(top)]
    gets = [refs.pop(0) for _ in range(top)]
    outs = [out_ref] + [refs.pop(0) for _ in range(top)]
    sends = [refs.pop(0) if halved[k] else None for k in range(top)]
    downs = [refs.pop(0) if halved[k] else None for k in range(top)]
    top_get, tots, tot_gets, decays, up_sems, down_sems, tot_sems = refs
    me = lax.axis_index("seq")
    bits = [lax.rem(me // (1 << k), 2) for k in range(levels)]
    partners = [me + (1 - 2 * bits[k]) * (1 << k) for k in range(levels)]
    barrier = pltpu.get_barrier_semaphore()
    for k in range(levels):
        pl.semaphore_signal(
            barrier, inc=1, device_id={"seq": partners[k]}, device_id_type=pl.DeviceIdType.MESH
        )
    pl.semaphore_wait(barrier, levels)
    span = width // CHUNKS

    def copy(source, target, send, receive, k):
        return pltpu.make_async_remote_copy(
            src_ref=source, dst_ref=target, send_sem=send, recv_sem=receive,
            device_id={"seq": partners[k]}, device_id_type=pl.DeviceIdType.MESH,
        )

    def half_at(k, which):
        size = sizes[k + 1]
        return pl.ds(pl.multiple_of(which * size, 8), size)

    def up_copy(k, c):
        cols = slice(c * span, (c + 1) * span)
        if k == top:
            source, target = aggs[k].at[bits[k], :, cols], top_get.at[:, cols]
        elif halved[k]:
            source, target = aggs[k].at[:, half_at(k, 1 - bits[k]), cols], gets[k].at[:, :, cols]
        else:
            source, target = aggs[k].at[:, :, cols], gets[k].at[:, :, cols]
        return copy(source, target, up_sems.at[0, k, c], up_sems.at[1, k, c], k)

    def down_copy(k, c):
        cols = slice(c * span, (c + 1) * span)
        return copy(sends[k].at[:, :, cols], downs[k].at[:, :, cols],
                    down_sems.at[0, k, c], down_sems.at[1, k, c], k)

    def tot_copy(k):
        return copy(tots.at[k], tot_gets.at[k], tot_sems.at[0, k], tot_sems.at[1, k], k)

    def tot_done(k):
        tot_copy(k).wait_recv()
        mine, other = tots[k], tot_gets[k]
        tots[k + 1] = mine + other
        left = jnp.where(bits[k] == 0, mine, other)
        right = jnp.where(bits[k] == 0, other, mine)
        hot = one_hot(TILE, head_size, width)
        decays[k, 0] = jnp.exp(spread_heads(left, hot))
        decays[k, 1] = jnp.exp(spread_heads(right, hot))

    def own(k, cols, part):
        if halved[k]:
            return aggs[k][part, half_at(k, bits[k]), cols]
        return aggs[k][part, :, cols]

    def finish_up(k, c):
        cols = slice(c * span, (c + 1) * span)
        up_copy(k, c).wait_recv()
        if c == 0:
            tot_done(k)
            if k + 1 < top:
                tot_copy(k + 1).start()
        first = bits[k] == 0
        s_mine, g_mine = own(k, cols, 0), own(k, cols, 1)
        s_got, g_got = gets[k][0, :, cols], gets[k][1, :, cols]
        s_left, s_right = jnp.where(first, s_mine, s_got), jnp.where(first, s_got, s_mine)
        g_left, g_right = jnp.where(first, g_mine, g_got), jnp.where(first, g_got, g_mine)
        aggs[k + 1][0, :, cols] = decays[k, 1, 0:1, cols] * s_left + s_right
        aggs[k + 1][1, :, cols] = g_left + decays[k, 0, 0:1, cols] * g_right
        up_copy(k + 1, c).start()

    def finish_top(c):
        cols = slice(c * span, (c + 1) * span)
        up_copy(top, c).wait_recv()
        got = top_get[:, cols]
        zero = jnp.zeros_like(got)
        outs[top][0, :, cols] = jnp.where(bits[top] == 1, got, zero)
        outs[top][1, :, cols] = jnp.where(bits[top] == 1, zero, got)
        if top > 0:
            step_down(top - 1, c)

    def step_down(k, c):
        cols = slice(c * span, (c + 1) * span)
        first = bits[k] == 0
        inc, outg = outs[k + 1][0, :, cols], outs[k + 1][1, :, cols]
        s_left = jnp.where(first, own(k, cols, 0), gets[k][0, :, cols])
        g_right = jnp.where(first, gets[k][1, :, cols], own(k, cols, 1))
        right_in = decays[k, 0, 0:1, cols] * inc + s_left
        left_out = decays[k, 1, 0:1, cols] * outg + g_right
        if halved[k]:
            sends[k][0, :, cols] = jnp.where(first, right_in, inc)
            sends[k][1, :, cols] = jnp.where(first, outg, left_out)
            down_copy(k, c).start()
            mine = half_at(k, bits[k])
        else:
            mine = slice(None)
        outs[k][0, mine, cols] = jnp.where(first, inc, right_in)
        outs[k][1, mine, cols] = jnp.where(first, left_out, outg)

    def finish_down(k, c):
        cols = slice(c * span, (c + 1) * span)
        if halved[k]:
            down_copy(k, c).wait_recv()
            outs[k][:, half_at(k, 1 - bits[k]), cols] = downs[k][:, :, cols]
        if k > 0:
            step_down(k - 1, c)

    tots[0] = total_ref[...]
    if top > 0:
        tot_copy(0).start()
    for c in range(CHUNKS):
        up_copy(0, c).start()
    stages = [functools.partial(finish_up, k) for k in range(top)]
    stages.append(finish_top)
    stages += [functools.partial(finish_down, k) for k in reversed(range(top))]
    for tick in range(len(stages) + CHUNKS - 1):
        for c in range(CHUNKS):
            if 0 <= tick - c < len(stages):
                stages[tick - c](c)
    for k in range(top):
        tot_copy(k).wait_send()
    for c in range(CHUNKS):
        for k in range(levels):
            up_copy(k, c).wait_send()
        for k in range(top):
            if halved[k]:
                down_copy(k, c).wait_send()


def scan_states(devices, heads, states, total):
    rows, width = states.shape[1], states.shape[2]
    levels, sizes, halved = scan_plan(devices, rows)
    top = levels - 1
    scratch = [pltpu.VMEM((2, sizes[k + 1], width), F32) for k in range(top)]
    scratch += [pltpu.VMEM((2, sizes[k + 1], width), F32) for k in range(top)]
    scratch += [pltpu.VMEM((2, sizes[k + 1], width), F32) for k in range(top)]
    for _ in range(2):
        scratch += [pltpu.VMEM((2, sizes[k + 1], width), F32) for k in range(top) if halved[k]]
    scratch += [
        pltpu.VMEM((sizes[top], width), F32),
        pltpu.VMEM((levels + 1, 8, TILE), F32),
        pltpu.VMEM((levels, 8, TILE), F32),
        pltpu.VMEM((levels, 2, 8, width), F32),
        pltpu.SemaphoreType.DMA((2, levels, CHUNKS)),
        pltpu.SemaphoreType.DMA((2, levels, CHUNKS)),
        pltpu.SemaphoreType.DMA((2, levels)),
    ]
    return pl.pallas_call(
        functools.partial(scan_kernel, devices, heads),
        out_shape=jax.ShapeDtypeStruct(states.shape, F32),
        in_specs=[VMEM, VMEM],
        out_specs=VMEM,
        scratch_shapes=scratch,
        compiler_params=pltpu.CompilerParams(
            collective_id=0, has_side_effects=True, vmem_limit_bytes=VMEM_LIMIT
        ),
        name="scan_states",
    )(states, total)


def after_kernel(
    values_ref, grad_ref, proj_ref, raw_ref, run_ref, u_ref, rate_ref, skip_ref,
    gu_ref, rows_ref, gscores_ref, ends_ref, wbc_ref, wdt_ref,
    gvalues_ref, glayer_ref, gproj_ref, small_ref,
):
    tokens, heads = raw_ref.shape
    width = values_ref.shape[1]
    head_size = width // heads
    state_dim = proj_ref.shape[1] // 2
    hot = one_hot(heads, head_size, width)
    raw, run = raw_ref[...], run_ref[...]
    rate = jnp.exp(rate_ref[...])
    step = jnp.maximum(raw, 0.0) + jnp.log1p(jnp.exp(-jnp.abs(raw)))
    total = run[tokens - 1 :, :]
    b_rows = proj_ref[:, :state_dim]
    c_rows = proj_ref[:, state_dim:]
    incoming, outgoing = ends_ref[0], ends_ref[1]
    inc_b, out_b = incoming.astype(BF16), outgoing.astype(BF16)
    values = values_ref[...].astype(F32)
    grad = grad_ref[...].astype(F32)
    step_wide = spread_heads(step, hot)
    lead_grad = spread_heads(jnp.exp(run), hot) * grad
    lead_b = lead_grad.astype(BF16)
    reads = head_sum(lead_grad * mm(c_rows, inc_b), hot)
    gscores = gscores_ref[...].astype(BF16)
    grad_c = mm_nt(lead_b, inc_b) + mm_tn(gscores, b_rows)
    tail_wide = spread_heads(jnp.exp(total - run), hot)
    back = tail_wide * mm(b_rows, out_b)
    grad_b = mm_nt((tail_wide * step_wide * values).astype(BF16), out_b) + mm(gscores, c_rows)
    gu = gu_ref[...]
    inner_cols = head_sum(u_ref[...].astype(F32) * gu, hot)
    back_sum = head_sum(values * back, hot)
    gu = gu + back
    gvalues_ref[...] = (step_wide * gu + spread_heads(skip_ref[...], hot) * grad).astype(BF16)
    grad_step = head_sum(values * gu, hot)
    cross = jnp.sum(incoming * outgoing, axis=0, keepdims=True)
    cross = head_sum(jnp.broadcast_to(cross, (8, width)), hot)[0:1]
    upper = triangle(tokens, lambda r, c: r <= c)
    lower = triangle(tokens, lambda r, c: r > c)
    inner = rows_ref[:, 0, :].T + reads - inner_cols
    grad_decay = exact_mm(upper, inner) + exact_mm(lower, step * back_sum) + jnp.exp(total) * cross
    sigmoid = 1.0 / (1.0 + jnp.exp(-raw))
    grad_raw = (grad_step - rate * grad_decay) * sigmoid
    gproj_ref[:, :state_dim] = grad_b.astype(BF16)
    gproj_ref[:, state_dim : 2 * state_dim] = grad_c.astype(BF16)
    gproj_ref[:, 2 * state_dim :] = grad_raw.astype(BF16)
    small_ref[...] = jnp.zeros_like(small_ref)
    small_ref[0:1] = jnp.sum(grad_raw, axis=0, keepdims=True)
    small_ref[1:2] = -rate * jnp.sum(grad_decay * step, axis=0, keepdims=True)
    glayer_ref[...] = (
        mm_nt(gproj_ref[:, : 2 * state_dim], wbc_ref[...])
        + mm_nt(grad_raw.astype(BF16), wdt_ref[...])
    ).astype(BF16)


def call(kernel, shapes, name, *operands):
    return pl.pallas_call(
        kernel,
        out_shape=[jax.ShapeDtypeStruct(shape, dtype) for shape, dtype in shapes],
        in_specs=[VMEM] * len(operands),
        out_specs=[VMEM] * len(shapes),
        compiler_params=pltpu.CompilerParams(vmem_limit_bytes=VMEM_LIMIT),
        name=name,
    )(*operands)


def local(layer_in, ssm_in, weight_bc, weight_dt, bias_dt, log_rate, skip_gain, grad_out):
    tokens, depth = layer_in.shape
    heads = log_rate.shape[0]
    width = ssm_in.shape[1]
    state_dim = weight_bc.shape[1] // 2
    head_size = width // heads
    devices = lax.axis_size("seq")
    bias, rate, gain = bias_dt[None, :], log_rate[None, :], skip_gain[None, :]
    proj, raw, run, run_rows, states, total, scores, skip_sum, u, runx = call(
        before_kernel,
        [
            ((tokens, 2 * state_dim), BF16),
            ((tokens, heads), F32),
            ((tokens, heads), F32),
            ((heads, 1, tokens), F32),
            ((2, state_dim, width), F32),
            ((8, TILE), F32),
            ((tokens, tokens), F32),
            ((8, heads), F32),
            ((tokens, width), BF16),
            ((tokens, heads * TILE), F32),
        ],
        "before",
        layer_in, ssm_in, weight_bc, weight_dt, bias, rate, grad_out,
    )
    ends = scan_states(devices, heads, states, total)
    gu, rows, gscores = call(
        functools.partial(inner_kernel, head_size),
        [((tokens, width), F32), ((heads, 1, tokens), F32), ((tokens, tokens), F32)],
        "inner",
        u, grad_out, scores, runx, run_rows,
    )
    grad_ssm_in, grad_layer_in, grad_proj, small = call(
        after_kernel,
        [
            ((tokens, width), BF16),
            ((tokens, depth), BF16),
            ((tokens, 2 * state_dim + heads), BF16),
            ((8, heads), F32),
        ],
        "after",
        ssm_in, grad_out, proj, raw, run, u, rate, gain, gu, rows, gscores, ends,
        weight_bc, weight_dt,
    )
    grad_rows = lax.dot_general(
        layer_in, grad_proj, (((0,), (0,)), ((), ())), preferred_element_type=F32
    )
    share = depth // devices
    columns = grad_rows.shape[1]
    small = jnp.concatenate([small[0:2], skip_sum[0:1]], axis=0)
    small = jnp.pad(small, ((0, 5), (0, columns - heads)))
    packed = jnp.concatenate(
        [
            grad_rows.reshape(devices, share, columns),
            jnp.broadcast_to(small[None], (devices, 8, columns)),
        ],
        axis=1,
    ).reshape(devices * (share + 8), columns)
    summed = lax.psum_scatter(packed, "seq", scatter_dimension=0, tiled=True)
    return (
        grad_ssm_in,
        grad_layer_in,
        summed[:share, : 2 * state_dim],
        summed[:share, 2 * state_dim :],
        summed[share, :heads],
        summed[share + 1, :heads],
        summed[share + 2, :heads],
    )


def solution(mesh):
    rows = P(("groups", "seq"), None)
    in_specs = (rows, rows, P(), P(), P(), P(), P(), rows)
    out_specs = (rows, rows, rows, rows, P("groups"), P("groups"), P("groups"))
    return jax.shard_map(local, mesh=mesh, in_specs=in_specs, out_specs=out_specs, check_vma=False)
```

time: 360 us -> 235 us (0.65); the launches traced: 353 us -> 234 us
  Pallas kernels: 0 us -> 92.3 us
  matrix products: 73.7 us -> 2.01 us
  blocking collectives: 42.5 us -> 0 us
  local copies, waits for them, and re-layouts: 54 us -> 12.6 us
  starting transfers between devices: 27.5 us -> 0.04 us
  other arithmetic: 26.8 us -> 4.31 us
  waiting for transfers between devices: 114 us -> 108 us
    all_to_all x3 -> x0, waiting for transfers between devices: 94.5 us -> none  [the longest x1 49.8 us: local(): lax.all_to_all(packed, 'seq', split_axis=1, concat_axis=1, tiled=True)]
    pallas_call x0 -> x4, Pallas kernels: none -> 92.3 us  [the longest x1 51.1 us: scan_states(): pl.pallas_call(functools.partial(scan_kernel, devices, heads), out_shape=...]
    unnamed x2, waiting for transfers between devices: 19.1 us -> 108 us
    dot_general x19 -> x0, matrix products: 71.4 us -> none  [the longest x2 29.6 us: block_pass(): inner = jnp.einsum('hts,shp->thp', mixing, values, precision=HIGHEST)]
    psum x1 -> x0, blocking collectives: 42.5 us -> none  [local(): lax.psum((jnp.sum(grad_step, axis=0), grad_log_rate, grad_skip_local), 's...]
    all_to_all x3 -> x0, starting transfers between devices: 27.3 us -> none  [the longest x1 13.4 us: local(): lax.all_to_all(joined, 'seq', split_axis=1, concat_axis=1, tiled=True)]
    reshape x6 -> x0, local copies, waits for them, and re-layouts: 15.1 us -> none  [the longest x2 5.71 us: local(): state_grad.reshape(heads, devices, share)]
    unnamed x51 -> x5, local copies, waits for them, and re-layouts: 13.6 us -> 3.94 us
  transfers between devices with their start and end apart: 4 -> 1, of which waited for: 3 -> 1; matrix products, arithmetic and copies ran while one was open for 14% -> 0% of each run, Pallas kernels for 0% -> 0%
where the time goes in v1:
time: 235 us; the launch traced here: 234 us
  waiting for transfers between devices  108 us (46%)
  Pallas kernels  92.3 us (39%)
  between operations  14.7 us (6%)
  local copies, waits for them, and re-layouts  12.6 us (5%)
  other arithmetic  4.31 us (2%)
    unnamed x2, waiting for transfers between devices  108 us
    pallas_call x1, Pallas kernels, scan_states(): pl.pallas_call(functools.partial(scan_kernel, devices, heads), out_shape=...  51.1 us
    pallas_call x3, Pallas kernels, call(): pl.pallas_call(kernel, out_shape=[jax.ShapeDtypeStruct(shape, dtype) for...  41.2 us
  transfers between devices with their start and end apart: 1, of which 1 were waited for; matrix products, arithmetic and copies ran while one was open for 0% of the time, Pallas kernels for 0%

profile of v1, /device:TPU:0, one launch (start us, length us, event | category | flops | bytes accessed | tf_op | source)
XLA Modules:
  0.0 234.5 jit_solution(8000979582085539322)
XLA Ops:
  7.2 0.0 all-reduce.4.cloned.1.call-start
  7.2 2.0 copy.23.wdt_ref
  9.2 13.5 %before.1 = (bf16[256,256]{1,0:T(8,128)(2,1)}, f32[256,40]{1,0:T(8,128)}, f32[256,40]{1,0:T(8,128)}, f32[40,1,256]{2,1,0:T(1,128)}, f32[2,128,2560]{2,1,0:T(8,12...) custom-call(bf16[256,2560]{1,0:T(8,128)(2,1)} %layer_ref.1, ...), custom_call_target="tpu_custom_call" | custom-call | tf_op jit(solution)/shard_map/before/pallas_call | solution.py:394
  22.8 0.7 slice.22
  23.5 51.1 %scan_states.1.ends_ref = f32[2,128,2560]{2,1,0:T(8,128)} custom-call(f32[2,128,2560]{2,1,0:T(8,128)} %get-tuple-element.34.states_ref, f32[8,128]{1,0:T(8,128)} %get-tuple-element.35.total_ref), custom_call_target="tpu_custom_call" | custom-call | tf_op jit(solution)/shard_map/scan_states/pallas_call | solution.py:325
  74.6 11.5 %inner.1 = (f32[256,2560]{1,0:T(8,128)}, f32[40,1,256]{2,1,0:T(1,128)}, f32[256,256]{1,0:T(8,128)}) custom-call(bf16[256,2560]{1,0:T(8,128)(2,1)} %get-tuple-element.27.u_ref, bf16[256,2560]{1,0:T(8,128)(2,1)} %grad_ref.5, f32[256,256]{1,0:T(8,128)} %get-tuple-element.28.scores_ref, f32[256,5120]{1,0:T(8,128)} %get-tuple-element.29.runx_ref, ...), custom_call_target="tpu_custom_call" | custom-call | tf_op jit(solution)/shard_map/inner/pallas_call | solution.py:394
  86.0 16.3 %after.1 = (bf16[256,2560]{1,0:T(8,128)(2,1)}, bf16[256,2560]{1,0:T(8,128)(2,1)}, bf16[256,296]{1,0:T(8,128)(2,1)}, f32[8,40]{1,0:T(8,128)}) custom-call(bf16[256,2560]{1,0:T(8,128)(2,1)} %values_ref.3, bf16[256,2560]{1,0:T(8,128)(2,1)} %grad_ref.5, bf16[256,256]{1,0:T(8,128)(2,1)} %get-tuple-element.24.proj_ref, f32[256,40]{1,0:T(8,128)} %get-tuple-element.25.raw_ref, ...), custom_call_target="tpu_custom_call" | custom-call | tf_op jit(solution)/shard_map/after/pallas_call | solution.py:394
  102.3 0.7 slice.21
  103.0 2.0 convolution_bitcast_fusion
  105.0 3.4 %copy.25 = f32[2560,296]{1,0:T(8,128)} copy(f32[2560,296]{0,1:T(8,128)S(1)} %convolution_bitcast_fusion) | data formatting | bytes 6062080 | tf_op jit(solution)/shard_map/dot_general | solution.py:448
  108.4 4.3 %pad_maximum_fusion = f32[16,168,296]{2,1,0:T(8,128)} fusion(f32[16,8,296]{2,1,0:T(8,128)S(1)} %broadcast_in_dim.18, f32[16,160,296]{2,1,0:T(8,128)} %bitcast.17), kind=kLoop, calls=%fused_computation.1 | loop fusion | flops 795648 | bytes 6365184 | tf_op jit(solution)/shard_map/concatenate | solution.py:455
  112.7 0.0 copy-start
  112.7 0.0 all-reduce.4.cloned.1.call-update
  112.7 0.6 copy-done
  113.4 0.6 dynamic-slice
  114.6 108.5 %all-reduce.4.cloned.1.call-done = f32[2688,296]{1,0:T(8,128)} async-done(((f32[2688,296]{1,0:T(8,128)}), f32[2688,296]{1,0:T(8,128)}) %all-reduce.4.cloned.1.call-update) | async-done | bytes 3182608
  223.1 1.0 dynamic-slice.3
  224.0 0.7 copy.26
  224.7 1.6 constant_dynamic-slice_fusion.2
  226.3 1.3 fusion
  (2 shorter events, 0.0 us)
Async XLA Ops:
  7.2 215.9 %all-reduce.4.cloned.1.call-start = ((), (), s32[]{:S(2)}) async-start(), calls=%async_computation | async-start | bytes 8257536
  112.7 0.7 copy-start
Sparse Core Ops, SparseCore 0:
  112.9 110.1 all-reduce.3

commit v2 on v1

--- a/solution.py
+++ b/solution.py
@@ -337,7 +337,7 @@
 
 def after_kernel(
     values_ref, grad_ref, proj_ref, raw_ref, run_ref, u_ref, rate_ref, skip_ref,
-    gu_ref, rows_ref, gscores_ref, ends_ref, wbc_ref, wdt_ref,
+    gu_ref, rows_ref, gscores_ref, ends_ref, wbc_ref, wdt_ref, skip_sum_ref,
     gvalues_ref, glayer_ref, gproj_ref, small_ref,
 ):
     tokens, heads = raw_ref.shape
@@ -382,12 +382,148 @@
     gproj_ref[:, state_dim : 2 * state_dim] = grad_c.astype(BF16)
     gproj_ref[:, 2 * state_dim :] = grad_raw.astype(BF16)
     small_ref[...] = jnp.zeros_like(small_ref)
-    small_ref[0:1] = jnp.sum(grad_raw, axis=0, keepdims=True)
-    small_ref[1:2] = -rate * jnp.sum(grad_decay * step, axis=0, keepdims=True)
+    small_ref[0:1, :heads] = jnp.sum(grad_raw, axis=0, keepdims=True)
+    small_ref[1:2, :heads] = -rate * jnp.sum(grad_decay * step, axis=0, keepdims=True)
+    small_ref[2:3, :heads] = skip_sum_ref[0:1]
     glayer_ref[...] = (
         mm_nt(gproj_ref[:, : 2 * state_dim], wbc_ref[...])
         + mm_nt(grad_raw.astype(BF16), wdt_ref[...])
     ).astype(BF16)
+
+
+def packing(depth, devices, heads):
+    share = depth // devices
+    lanes = TILE // heads
+    group = -(-share // (8 * lanes)) * 8
+    return share, lanes, group
+
+
+def reduce_kernel(devices, heads, layer_ref, gproj_ref, small_ref,
+                  gbc_ref, gdt_ref, gbias_ref, grate_ref, gskip_ref, *refs):
+    depth = layer_ref.shape[1]
+    share, lanes, group = packing(depth, devices, heads)
+    levels = devices.bit_length() - 1
+    wide = gbc_ref.shape[1]
+    planes = wide // TILE + 1
+    refs = list(refs)
+    sems = refs.pop()
+    sums = [refs.pop(0) for _ in range(planes)]
+    gets = [[refs.pop(0) for _ in range(levels)] for _ in range(planes)]
+    units = [share] * (planes - 1) + [group + 8]
+    me = lax.axis_index("seq")
+    bits = [lax.rem(me // (1 << k), 2) for k in range(levels)]
+    partners = [me + (1 - 2 * bits[k]) * (1 << k) for k in range(levels)]
+    offsets = [0]
+    for k in range(levels):
+        offsets.append(offsets[k] + bits[k] * (devices >> (k + 1)))
+    barrier = pltpu.get_barrier_semaphore()
+    for k in range(levels):
+        pl.semaphore_signal(
+            barrier, inc=1, device_id={"seq": partners[k]}, device_id_type=pl.DeviceIdType.MESH
+        )
+    pl.semaphore_wait(barrier, levels)
+    places = [
+        sum(((shard >> k) & 1) * (devices >> (k + 1)) for k in range(levels))
+        for shard in range(devices)
+    ]
+
+    def half(k, plane, which):
+        size = (devices >> (k + 1)) * units[plane]
+        start = (offsets[k] + which * (devices >> (k + 1))) * units[plane]
+        return pl.ds(pl.multiple_of(start, 8), size)
+
+    def copy(k, plane):
+        return pltpu.make_async_remote_copy(
+            src_ref=sums[plane].at[half(k, plane, 1 - bits[k])],
+            dst_ref=gets[plane][k],
+            send_sem=sems.at[0, k, plane],
+            recv_sem=sems.at[1, k, plane],
+            device_id={"seq": partners[k]},
+            device_id_type=pl.DeviceIdType.MESH,
+        )
+
+    layer = layer_ref[...]
+    rows_bc = mm_tn(layer, gproj_ref[:, :wide])
+    for plane in range(planes - 1):
+        for shard in range(devices):
+            sums[plane][places[shard] * share : (places[shard] + 1) * share] = rows_bc[
+                shard * share : (shard + 1) * share, plane * TILE : (plane + 1) * TILE
+            ]
+        copy(0, plane).start()
+    row = lax.broadcasted_iota(jnp.int32, (heads, lanes * TILE), 0)
+    col = lax.broadcasted_iota(jnp.int32, (heads, lanes * TILE), 1)
+    shift = jnp.zeros(row.shape, F32)
+    for j in range(lanes):
+        shift = jnp.where(col == row + j * (TILE + heads), 1.0, shift)
+    moved = mm(gproj_ref[:, wide:], shift.astype(BF16)).astype(BF16)
+    rows_dt = mm_tn(layer, moved)
+    unit = group + 8
+    for shard in range(devices):
+        start = places[shard] * unit
+        packed = jnp.zeros((group, TILE), F32)
+        for j in range(lanes):
+            count = min(share - j * group, group)
+            if count <= 0:
+                continue
+            part = rows_dt[
+                shard * share + j * group : shard * share + j * group + count,
+                j * TILE : (j + 1) * TILE,
+            ]
+            if count < group:
+                part = jnp.concatenate([part, jnp.zeros((group - count, TILE), F32)], axis=0)
+            packed = packed + part
+        sums[-1][start : start + group] = packed
+        sums[-1][start + group : start + unit] = small_ref[...]
+    copy(0, planes - 1).start()
+
+    for tick in range(levels + planes - 1):
+        for plane in range(planes):
+            k = tick - plane
+            if not 0 <= k < levels:
+                continue
+            copy(k, plane).wait_recv()
+            mine = half(k, plane, bits[k])
+            sums[plane][mine] = sums[plane][mine] + gets[plane][k][...]
+            if k + 1 < levels:
+                copy(k + 1, plane).start()
+    for plane in range(planes - 1):
+        start = pl.multiple_of(offsets[levels] * share, 8)
+        gbc_ref[:, plane * TILE : (plane + 1) * TILE] = sums[plane][pl.ds(start, share)]
+    last = sums[-1][pl.ds(pl.multiple_of(offsets[levels] * unit, 8), unit)]
+    for j in range(lanes):
+        count = min(share - j * group, group)
+        if count > 0:
+            gdt_ref[j * group : j * group + count] = last[:count, j * heads : (j + 1) * heads]
+    gbias_ref[...] = last[group : group + 1, :heads]
+    grate_ref[...] = last[group + 1 : group + 2, :heads]
+    gskip_ref[...] = last[group + 2 : group + 3, :heads]
+    for plane in range(planes):
+        for k in range(levels):
+            copy(k, plane).wait_send()
+
+
+def reduce_rows(devices, heads, layer_in, grad_proj, small):
+    depth = layer_in.shape[1]
+    wide = grad_proj.shape[1] - heads
+    share, lanes, group = packing(depth, devices, heads)
+    levels = devices.bit_length() - 1
+    units = [share] * (wide // TILE) + [group + 8]
+    scratch = [pltpu.VMEM((devices * unit, TILE), F32) for unit in units]
+    for unit in units:
+        scratch += [pltpu.VMEM(((devices >> (k + 1)) * unit, TILE), F32) for k in range(levels)]
+    scratch.append(pltpu.SemaphoreType.DMA((2, levels, len(units))))
+    shapes = [(share, wide), (share, heads), (1, heads), (1, heads), (1, heads)]
+    return pl.pallas_call(
+        functools.partial(reduce_kernel, devices, heads),
+        out_shape=[jax.ShapeDtypeStruct(shape, F32) for shape in shapes],
+        in_specs=[VMEM] * 3,
+        out_specs=[VMEM] * 5,
+        scratch_shapes=scratch,
+        compiler_params=pltpu.CompilerParams(
+            collective_id=1, has_side_effects=True, vmem_limit_bytes=VMEM_LIMIT
+        ),
+        name="reduce_rows",
+    )(layer_in, grad_proj, small)
 
 
 def call(kernel, shapes, name, *operands):
@@ -439,35 +575,23 @@
             ((tokens, width), BF16),
             ((tokens, depth), BF16),
             ((tokens, 2 * state_dim + heads), BF16),
-            ((8, heads), F32),
+            ((8, TILE), F32),
         ],
         "after",
         ssm_in, grad_out, proj, raw, run, u, rate, gain, gu, rows, gscores, ends,
-        weight_bc, weight_dt,
+        weight_bc, weight_dt, skip_sum,
     )
-    grad_rows = lax.dot_general(
-        layer_in, grad_proj, (((0,), (0,)), ((), ())), preferred_element_type=F32
+    grad_bc, grad_dt, grad_bias, grad_rate, grad_skip = reduce_rows(
+        devices, heads, layer_in, grad_proj, small
     )
-    share = depth // devices
-    columns = grad_rows.shape[1]
-    small = jnp.concatenate([small[0:2], skip_sum[0:1]], axis=0)
-    small = jnp.pad(small, ((0, 5), (0, columns - heads)))
-    packed = jnp.concatenate(
-        [
-            grad_rows.reshape(devices, share, columns),
-            jnp.broadcast_to(small[None], (devices, 8, columns)),
-        ],
-        axis=1,
-    ).reshape(devices * (share + 8), columns)
-    summed = lax.psum_scatter(packed, "seq", scatter_dimension=0, tiled=True)
     return (
         grad_ssm_in,
         grad_layer_in,
-        summed[:share, : 2 * state_dim],
-        summed[:share, 2 * state_dim :],
-        summed[share, :heads],
-        summed[share + 1, :heads],
-        summed[share + 2, :heads],
+        grad_bc,
+        grad_dt,
+        grad_bias[0],
+        grad_rate[0],
+        grad_skip[0],
     )
 
 

time: 235 us -> 139 us (0.59)
  waiting for transfers between devices: 108 us -> 0 us
  Pallas kernels: 92.3 us -> 129 us
  between operations: 14.7 us -> 0.65 us
  other arithmetic: 4.31 us -> 0 us
  local copies, waits for them, and re-layouts: 12.6 us -> 8.64 us
    unnamed x2 -> x0, waiting for transfers between devices: 108 us -> none
    pallas_call x0 -> x1, Pallas kernels: none -> 36.8 us  [reduce_rows(): pl.pallas_call(functools.partial(reduce_kernel, devices, heads), out_shap...]
    unnamed x5 -> x6, local copies, waits for them, and re-layouts: 3.94 us -> 8.64 us
    concatenate x2 -> x0, other arithmetic: 4.31 us -> none  [the longest x1 4.3 us: local(): jnp.concatenate([grad_rows.reshape(devices, share, columns), jnp.broadcas...]
    slice x4 -> x0, local copies, waits for them, and re-layouts: 3.94 us -> none  [the longest x1 1.59 us: local(): summed[:share, :2 * state_dim]]
    dot_general x1 -> x0, local copies, waits for them, and re-layouts: 3.39 us -> none  [local(): lax.dot_general(layer_in, grad_proj, (((0,), (0,)), ((), ())), preferred_...]
  transfers between devices with their start and end apart: 1 -> 0, of which waited for: 1 -> 0; matrix products, arithmetic and copies ran while one was open for 0% -> 0% of each run, Pallas kernels for 0% -> 0%
where the time goes in v2:
time: 139 us; the launch traced here: 138 us
  Pallas kernels  129 us (93%)
  local copies, waits for them, and re-layouts  8.64 us (6%)
    pallas_call x1, Pallas kernels, scan_states(): pl.pallas_call(functools.partial(scan_kernel, devices, heads), out_shape=...  51.1 us
    pallas_call x3, Pallas kernels, call(): pl.pallas_call(kernel, out_shape=[jax.ShapeDtypeStruct(shape, dtype) for...  41.1 us
    pallas_call x1, Pallas kernels, reduce_rows(): pl.pallas_call(functools.partial(reduce_kernel, devices, heads), out_shap...  36.8 us
    unnamed x6, local copies, waits for them, and re-layouts  8.64 us

profile of v2, /device:TPU:0, one launch (start us, length us, event | category | flops | bytes accessed | tf_op | source)
XLA Modules:
  0.0 138.4 jit_solution(16521034174202706634)
XLA Ops:
  0.6 2.0 %copy.15.wdt_ref = bf16[2560,40]{1,0:T(8,128)(2,1)} copy(bf16[2560,40]{0,1:T(8,128)(2,1)} %param.11) | data formatting | bytes 409600 | tf_op args[3]
  2.7 13.5 %before.1 = (bf16[256,256]{1,0:T(8,128)(2,1)}, f32[256,40]{1,0:T(8,128)}, f32[256,40]{1,0:T(8,128)}, f32[40,1,256]{2,1,0:T(1,128)}, f32[2,128,2560]{2,1,0:T(8,12...) custom-call(bf16[256,2560]{1,0:T(8,128)(2,1)} %layer_ref.3, ...), custom_call_target="tpu_custom_call" | custom-call | tf_op jit(solution)/shard_map/before/pallas_call | solution.py:530
  16.2 51.1 %scan_states.1.ends_ref = f32[2,128,2560]{2,1,0:T(8,128)} custom-call(f32[2,128,2560]{2,1,0:T(8,128)} %get-tuple-element.39.states_ref, f32[8,128]{1,0:T(8,128)} %get-tuple-element.40.total_ref), custom_call_target="tpu_custom_call" | custom-call | tf_op jit(solution)/shard_map/scan_states/pallas_call | solution.py:325
  67.3 11.3 %inner.1 = (f32[256,2560]{1,0:T(8,128)}, f32[40,1,256]{2,1,0:T(1,128)}, f32[256,256]{1,0:T(8,128)}) custom-call(bf16[256,2560]{1,0:T(8,128)(2,1)} %get-tuple-element.32.u_ref, bf16[256,2560]{1,0:T(8,128)(2,1)} %grad_ref.5, f32[256,256]{1,0:T(8,128)} %get-tuple-element.33.scores_ref, f32[256,5120]{1,0:T(8,128)} %get-tuple-element.34.runx_ref, ...), custom_call_target="tpu_custom_call" | custom-call | tf_op jit(solution)/shard_map/inner/pallas_call | solution.py:530
  78.6 16.3 %after.1 = (bf16[256,2560]{1,0:T(8,128)(2,1)}, bf16[256,2560]{1,0:T(8,128)(2,1)}, bf16[256,296]{1,0:T(8,128)(2,1)}, f32[8,128]{1,0:T(8,128)}) custom-call(bf16[256,2560]{1,0:T(8,128)(2,1)} %values_ref.3, bf16[256,2560]{1,0:T(8,128)(2,1)} %grad_ref.5, bf16[256,256]{1,0:T(8,128)(2,1)} %get-tuple-element.29.proj_ref, f32[256,40]{1,0:T(8,128)} %get-tuple-element.30.raw_ref, ...), custom_call_target="tpu_custom_call" | custom-call | tf_op jit(solution)/shard_map/after/pallas_call | solution.py:530
  94.9 36.8 %reduce_rows.1 = (f32[160,256]{1,0:T(8,128)}, f32[160,40]{1,0:T(8,128)}, f32[1,40]{1,0:T(1,128)}, f32[1,40]{1,0:T(1,128)}, f32[1,40]{1,0:T(1,128)}) custom-call(bf16[256,2560]{1,0:T(8,128)(2,1)} %layer_ref.3, bf16[256,296]{1,0:T(8,128)(2,1)} %get-tuple-element.44.gproj_ref, f32[8,128]{1,0:T(8,128)} %get-tuple-element.45.small_ref), custom_call_target="tpu_custom_call" | custom-call | tf_op jit(solution)/shard_map/reduce_rows/pallas_call | solution.py:516
  131.7 1.6 %copy.17 = f32[160,40]{0,1:T(8,128)} copy(f32[160,40]{1,0:T(8,128)} %get-tuple-element.54) | data formatting | bytes 51200
  133.3 1.6 %copy.22 = f32[160,256]{1,0:T(8,128)} copy(f32[160,256]{1,0:T(8,128)} %get-tuple-element.67) | data formatting | bytes 327680
  134.9 1.1 copy.23
  136.1 1.2 copy.24
  137.3 1.1 copy.25

commit v3 on v2

--- a/solution.py
+++ b/solution.py
@@ -78,7 +78,7 @@
     b_rows = proj[:, :state_dim]
     c_rows = proj[:, state_dim:]
     scores_ref[...] = mm_nt(b_rows, c_rows)
-    raw = mm(layer, wdt_ref[...]) + bias_ref[...]
+    raw = mm_nt(layer, wdt_ref[...]) + bias_ref[...]
     raw_ref[...] = raw
     step = jnp.maximum(raw, 0.0) + jnp.log1p(jnp.exp(-jnp.abs(raw)))
     decay = -jnp.exp(rate_ref[...]) * step
@@ -104,7 +104,7 @@
     runx_ref[...] = spread_heads(run, wide)
 
 
-def inner_pair(pair, values_ref, u_ref, grad_ref, scores_ref, runx_ref, run_rows_ref,
+def inner_pair(pair, u_ref, grad_ref, scores_ref, runx_ref, run_rows_ref,
                gu_ref, rows_ref, gscores_ref, head_size):
     tokens = u_ref.shape[0]
     blocks = tokens // TILE
@@ -142,18 +142,6 @@
         gu_ref[s * TILE : (s + 1) * TILE, cols] = gus[s]
 
 
-def inner_kernel(head_size, u_ref, grad_ref, scores_ref, runx_ref, run_rows_ref,
-                 gu_ref, rows_ref, gscores_ref):
-    gscores_ref[...] = jnp.zeros_like(gscores_ref)
-
-    def body(pair, _):
-        inner_pair(pair, None, u_ref, grad_ref, scores_ref, runx_ref, run_rows_ref,
-                   gu_ref, rows_ref, gscores_ref, head_size)
-        return 0
-
-    lax.fori_loop(0, u_ref.shape[1] // TILE, body, 0)
-
-
 def scan_plan(devices, rows):
     levels = devices.bit_length() - 1
     sizes, halved = [rows], []
@@ -164,7 +152,8 @@
     return levels, sizes, halved
 
 
-def scan_kernel(devices, heads, states_ref, total_ref, out_ref, *refs):
+def scan_kernel(devices, heads, states_ref, total_ref, u_ref, grad_ref, scores_ref, runx_ref,
+                run_rows_ref, out_ref, gu_ref, rows_ref, gscores_ref, *refs):
     rows, width = states_ref.shape[1], states_ref.shape[2]
     head_size = width // heads
     levels, sizes, halved = scan_plan(devices, rows)
@@ -290,7 +279,17 @@
     stages = [functools.partial(finish_up, k) for k in range(top)]
     stages.append(finish_top)
     stages += [functools.partial(finish_down, k) for k in reversed(range(top))]
-    for tick in range(len(stages) + CHUNKS - 1):
+    gscores_ref[...] = jnp.zeros_like(gscores_ref)
+
+    def body(pair, _):
+        inner_pair(pair, u_ref, grad_ref, scores_ref, runx_ref, run_rows_ref,
+                   gu_ref, rows_ref, gscores_ref, head_size)
+        return 0
+
+    pairs = width // TILE
+    ticks = len(stages) + CHUNKS - 1
+    for tick in range(ticks):
+        lax.fori_loop(tick * pairs // ticks, (tick + 1) * pairs // ticks, body, 0)
         for c in range(CHUNKS):
             if 0 <= tick - c < len(stages):
                 stages[tick - c](c)
@@ -304,7 +303,7 @@
                 down_copy(k, c).wait_send()
 
 
-def scan_states(devices, heads, states, total):
+def scan_states(devices, heads, states, total, u, grad, scores, runx, run_rows):
     rows, width = states.shape[1], states.shape[2]
     levels, sizes, halved = scan_plan(devices, rows)
     top = levels - 1
@@ -324,15 +323,18 @@
     ]
     return pl.pallas_call(
         functools.partial(scan_kernel, devices, heads),
-        out_shape=jax.ShapeDtypeStruct(states.shape, F32),
-        in_specs=[VMEM, VMEM],
-        out_specs=VMEM,
+        out_shape=[
+            jax.ShapeDtypeStruct(shape, F32)
+            for shape in (states.shape, u.shape, run_rows.shape, scores.shape)
+        ],
+        in_specs=[VMEM] * 7,
+        out_specs=[VMEM] * 4,
         scratch_shapes=scratch,
         compiler_params=pltpu.CompilerParams(
             collective_id=0, has_side_effects=True, vmem_limit_bytes=VMEM_LIMIT
         ),
         name="scan_states",
-    )(states, total)
+    )(states, total, u, grad, scores, runx, run_rows)
 
 
 def after_kernel(
@@ -387,7 +389,7 @@
     small_ref[2:3, :heads] = skip_sum_ref[0:1]
     glayer_ref[...] = (
         mm_nt(gproj_ref[:, : 2 * state_dim], wbc_ref[...])
-        + mm_nt(grad_raw.astype(BF16), wdt_ref[...])
+        + mm(grad_raw.astype(BF16), wdt_ref[...])
     ).astype(BF16)
 
 
@@ -544,6 +546,7 @@
     state_dim = weight_bc.shape[1] // 2
     head_size = width // heads
     devices = lax.axis_size("seq")
+    narrow = weight_dt.T
     bias, rate, gain = bias_dt[None, :], log_rate[None, :], skip_gain[None, :]
     proj, raw, run, run_rows, states, total, scores, skip_sum, u, runx = call(
         before_kernel,
@@ -560,14 +563,10 @@
             ((tokens, heads * TILE), F32),
         ],
         "before",
-        layer_in, ssm_in, weight_bc, weight_dt, bias, rate, grad_out,
+        layer_in, ssm_in, weight_bc, narrow, bias, rate, grad_out,
     )
-    ends = scan_states(devices, heads, states, total)
-    gu, rows, gscores = call(
-        functools.partial(inner_kernel, head_size),
-        [((tokens, width), F32), ((heads, 1, tokens), F32), ((tokens, tokens), F32)],
-        "inner",
-        u, grad_out, scores, runx, run_rows,
+    ends, gu, rows, gscores = scan_states(
+        devices, heads, states, total, u, grad_out, scores, runx, run_rows
     )
     grad_ssm_in, grad_layer_in, grad_proj, small = call(
         after_kernel,
@@ -579,7 +578,7 @@
         ],
         "after",
         ssm_in, grad_out, proj, raw, run, u, rate, gain, gu, rows, gscores, ends,
-        weight_bc, weight_dt, skip_sum,
+        weight_bc, narrow, skip_sum,
     )
     grad_bc, grad_dt, grad_bias, grad_rate, grad_skip = reduce_rows(
         devices, heads, layer_in, grad_proj, small

time: 139 us -> 128 us (0.921)
  Pallas kernels: 129 us -> 121 us
  local copies, waits for them, and re-layouts: 8.64 us -> 6.66 us
    pallas_call x3 -> x2, Pallas kernels: 41.1 us -> 29.4 us  [call(): pl.pallas_call(kernel, out_shape=[jax.ShapeDtypeStruct(shape, dtype) for...]
    pallas_call x1, Pallas kernels: 51.1 us -> 54.5 us  [scan_states(): pl.pallas_call(functools.partial(scan_kernel, devices, heads), out_shape=...]
    unnamed x6 -> x5, local copies, waits for them, and re-layouts: 8.64 us -> 6.66 us
where the time goes in v3:
time: 128 us
  Pallas kernels  121 us (95%)
  local copies, waits for them, and re-layouts  6.66 us (5%)
    pallas_call x1, Pallas kernels, scan_states(): pl.pallas_call(functools.partial(scan_kernel, devices, heads), out_shape=...  54.5 us
    pallas_call x1, Pallas kernels, reduce_rows(): pl.pallas_call(functools.partial(reduce_kernel, devices, heads), out_shap...  36.7 us
    pallas_call x2, Pallas kernels, call(): pl.pallas_call(kernel, out_shape=[jax.ShapeDtypeStruct(shape, dtype) for...  29.4 us
    unnamed x5, local copies, waits for them, and re-layouts  6.66 us

profile of v3, /device:TPU:0, one launch (start us, length us, event | category | flops | bytes accessed | tf_op | source)
XLA Modules:
  0.0 128.0 jit_solution(9145243835186657560)
XLA Ops:
  0.6 13.2 %before.1 = (bf16[256,256]{1,0:T(8,128)(2,1)}, f32[256,40]{1,0:T(8,128)}, f32[256,40]{1,0:T(8,128)}, f32[40,1,256]{2,1,0:T(1,128)}, f32[2,128,2560]{2,1,0:T(8,12...) custom-call(bf16[256,2560]{1,0:T(8,128)(2,1)} %layer_ref.3, ...), custom_call_target="tpu_custom_call" | custom-call | tf_op jit(solution)/shard_map/before/pallas_call | solution.py:532
  13.9 54.5 %scan_states.1 = (f32[2,128,2560]{2,1,0:T(8,128)}, f32[256,2560]{1,0:T(8,128)}, f32[40,1,256]{2,1,0:T(1,128)}, f32[256,256]{1,0:T(8,128)}) custom-call(f32[2,128,2560]{2,1,0:T(8,128)} %get-tuple-element.34.states_ref, f32[8,128]{1,0:T(8,128)} %get-tuple-element.35.total_ref, bf16[256,2560]{1,0:T(8,128)(2,1)} %get-tuple-element.33.u_ref, ...), custom_call_target="tpu_custom_call" | custom-call | tf_op jit(solution)/shard_map/scan_states/pallas_call | solution.py:324
  68.4 16.2 %after.1 = (bf16[256,2560]{1,0:T(8,128)(2,1)}, bf16[256,2560]{1,0:T(8,128)(2,1)}, bf16[256,296]{1,0:T(8,128)(2,1)}, f32[8,128]{1,0:T(8,128)}) custom-call(bf16[256,2560]{1,0:T(8,128)(2,1)} %values_ref.3, bf16[256,2560]{1,0:T(8,128)(2,1)} %grad_ref.5, bf16[256,256]{1,0:T(8,128)(2,1)} %get-tuple-element.30.proj_ref, f32[256,40]{1,0:T(8,128)} %get-tuple-element.31.raw_ref, ...), custom_call_target="tpu_custom_call" | custom-call | tf_op jit(solution)/shard_map/after/pallas_call | solution.py:532
  84.6 36.7 %reduce_rows.1 = (f32[160,256]{1,0:T(8,128)}, f32[160,40]{1,0:T(8,128)}, f32[1,40]{1,0:T(1,128)}, f32[1,40]{1,0:T(1,128)}, f32[1,40]{1,0:T(1,128)}) custom-call(bf16[256,2560]{1,0:T(8,128)(2,1)} %layer_ref.3, bf16[256,296]{1,0:T(8,128)(2,1)} %get-tuple-element.46.gproj_ref, f32[8,128]{1,0:T(8,128)} %get-tuple-element.47.small_ref), custom_call_target="tpu_custom_call" | custom-call | tf_op jit(solution)/shard_map/reduce_rows/pallas_call | solution.py:518
  121.4 1.6 %copy.15 = f32[160,40]{0,1:T(8,128)} copy(f32[160,40]{1,0:T(8,128)} %get-tuple-element.56) | data formatting | bytes 51200
  122.9 1.6 %copy.20 = f32[160,256]{1,0:T(8,128)} copy(f32[160,256]{1,0:T(8,128)} %get-tuple-element.69) | data formatting | bytes 327680
  124.5 1.2 copy.21
  125.7 1.2 copy.22
  126.9 1.1 copy.23
